TPU v7x, 32 devices: a whole 2x2x4 slice. The times are simulated.
32 devices in a mesh: groups: 2 (over y), patch: 8 (over z, x), head: 2 (over core).
Axes of the slice: x: 2, y: 2, z: 4, core: 2. Of those that a mesh axis runs over, the one named last changes fastest.
Arguments:
- queries: bfloat16 [2, 256, 1536], P(None, ('groups', 'patch'), 'head'), parts along dimension 1, may hold values from -15 to 15
- stale_pairs: bfloat16 [2, 320, 1536], P(None, ('groups', 'patch'), 'head'), parts along dimension 1, may hold values from -6 to 6
- step_pairs: bfloat16 [2, 2, 320, 1536], P(None, None, ('groups', 'patch'), 'head'), parts along dimension 2, may hold values from -6 to 6
- hidden: bfloat16 [256, 3072], P(('groups', 'patch'), 'head'), parts along dimension 0, may hold values from -3 to 3
- out_weight: bfloat16 [1536, 3072], P('head'), may hold values from -0.15625 to 0.15625
- gate_table: bfloat16 [28, 3072], replicated, may hold values from -4 to 4
- t_index: int32 [4], P('groups'), parts along dimension 0, may hold values from 0 to 27
- text_len: int32 [2], P('groups'), parts along dimension 0, may hold values from 1 to 32
Outputs:
- final_latents: bfloat16 [256, 3072], P(('groups', 'patch', 'head')), parts along dimension 0
There are 2 independent parts, one for each index of `groups`. A program takes and returns all parts, laid end to end along the dimension named above; an argument that names none is the same for every part. Nothing has to cross between parts.
All inputs are finite; a program needn't handle non-finite values.
Results may differ from a plain program's by a relative error of at most 0.0065.
Values may be sent and summed in bfloat16 or wider, within the bound.
A program may use at most 128 MiB of HBM per device.

v0:
```python
import jax
import jax.numpy as jnp
from jax import lax
from jax.sharding import PartitionSpec as P

HDIM = 128


def attend(query_rows, key_rows, value_rows, usable):
    count = query_rows.shape[0]
    total = key_rows.shape[0]
    heads_here = query_rows.shape[1] // HDIM
    qs = query_rows.reshape(count, heads_here, HDIM)
    ks = key_rows.reshape(total, heads_here, HDIM)
    vs = value_rows.reshape(total, heads_here, HDIM)
    scores = jnp.einsum("qhd,khd->hqk", qs, ks, preferred_element_type=jnp.float32) * (
        1.0 / HDIM**0.5
    )
    scores = jnp.where(usable[None, None, :], scores, jnp.float32(-1e30))
    top = jnp.max(scores, axis=2, keepdims=True)
    expo = jnp.exp(scores - top)
    weights = (expo / jnp.sum(expo, axis=2, keepdims=True)).astype(jnp.bfloat16)
    mixed = jnp.einsum("hqk,khd->qhd", weights, vs, preferred_element_type=jnp.float32)
    return mixed.reshape(count, heads_here * HDIM).astype(jnp.bfloat16)


def per_device(queries, stale_pairs, step_pairs, hidden, out_weight, gate_table, t_index, text_len):
    strip_rows = stale_pairs.shape[1]
    lat_rows = queries.shape[1]
    text_rows = strip_rows - lat_rows
    strip_count = lax.axis_size("patch")
    strip_index = lax.axis_index("patch")
    head_index = lax.axis_index("head")
    head_count = lax.axis_size("head")
    total = strip_rows * strip_count
    positions = jnp.arange(total, dtype=jnp.int32)
    within = positions % strip_rows
    holder = positions // strip_rows
    usable = (within < lat_rows) | (holder * text_rows + within - lat_rows < text_len[0])
    old_sets = lax.all_gather(stale_pairs, "patch", axis=1, tiled=True)
    first_sets = lax.all_gather(step_pairs[0], "patch", axis=1, tiled=True)
    remote_sets = (old_sets, first_sets)
    model_width = out_weight.shape[1]
    col_width = model_width // head_count

    def project(section):
        pairs = lax.dynamic_update_slice_in_dim(
            remote_sets[section], step_pairs[section], strip_index * strip_rows, axis=1
        )
        attended = attend(queries[section], pairs[0], pairs[1], usable)
        return jnp.dot(attended, out_weight, preferred_element_type=jnp.float32)

    state = hidden.astype(jnp.float32)
    first_proj = lax.psum_scatter(
        project(0).astype(jnp.bfloat16), "head", scatter_dimension=1, tiled=True
    ).astype(jnp.float32)
    gate_row = gate_table[t_index[0]].astype(jnp.float32)
    state = (
        state
        + lax.dynamic_slice_in_dim(gate_row, head_index * col_width, col_width, 0)[None, :]
        * first_proj
    )
    moved = lax.all_to_all(state, "head", split_axis=0, concat_axis=1, tiled=True)
    last_proj = lax.psum_scatter(project(1), "head", scatter_dimension=0, tiled=True)
    gate_full = gate_table[t_index[1]].astype(jnp.float32)
    return (moved + gate_full[None, :] * last_proj).astype(jnp.bfloat16)


def solution(mesh):
    return jax.shard_map(
        per_device,
        mesh=mesh,
        in_specs=(
            P(None, ("groups", "patch"), "head"),
            P(None, ("groups", "patch"), "head"),
            P(None, None, ("groups", "patch"), "head"),
            P(("groups", "patch"), "head"),
            P("head", None),
            P(),
            P("groups"),
            P("groups"),
        ),
        out_specs=P(("groups", "patch", "head"), None),
        check_vma=False,
    )
```

profile of v0, /device:TPU:0, one launch (start us, length us, event | category | flops | bytes accessed | tf_op | source)
XLA Modules:
  0.0 112.2 jit_solution(2523433137556579357)
XLA Ops:
  6.5 0.9 slice_bitcast_fusion
  7.4 33.0 %all-gather = bf16[1,2,160,768]{3,1,0,2:T(2,128)(2,1)S(1)} all-gather(bf16[1,2,20,768]{3,1,0,2:T(2,128)(2,1)S(1)} %slice_bitcast_fusion), channel_id=2, replica_groups=mesh['groups'=2,'patch'=8,'head'=2] {'patch'}, dimensions={2}, use_global_device_ids=true | all-gather | bytes 552960 | tf_op jit(solution)/shard_map/all_gather | solution.py:41
  40.4 31.4 %all_gather.6 = bf16[2,160,768]{2,0,1:T(2,128)(2,1)S(1)} all-gather(bf16[2,20,768]{2,0,1:T(2,128)(2,1)} %param.9), channel_id=1, replica_groups=mesh['groups'=2,'patch'=8,'head'=2] {'patch'}, dimensions={1}, use_global_device_ids=true | all-gather | bytes 552960 | tf_op jit(solution)/shard_map/all_gather | solution.py:40
  71.7 0.8 fusion.33
  72.5 0.1 reshape_squeeze.20
  73.2 1.0 bitcast_dynamic-update-slice_fusion
  74.2 5.2 %slice_reduce_fusion.1 = (bf16[160,768]{1,0:T(8,128)(2,1)S(1)}, bf16[160,768]{1,0:T(8,128)(2,1)S(1)}, bf16[160,768]{1,0:T(8,128)(2,1)S(1)}, bf16[160,768]{1,0:T(8,128)(2,1)S(1)}) fusion(bf16[2,160,768]{2,0,1:T(2,128)(2,1)S(1)} %get-tuple-element.9, bf16[2,160,768]{2,0,1:T(2,128)(2,1)S(1)} %get-tuple-element.10), kind=kLoop, calls=%fused_computation.18 | loop fusion | bytes 1966080 | tf_op jit(solution)/shard_map/slice | solution.py:50
  79.3 0.4 fusion.35
  79.8 0.2 fusion.10
  80.0 3.7 %convolution_convert_fusion = bf16[16,3072]{1,0:T(8,128)(2,1)} fusion(bf16[768,3072]{1,0:T(8,128)(2,1)} %param.12, bf16[6,2,8,128]{3,2,1,0:T(8,128)(2,1)S(1)} %fusion.10), kind=kOutput, calls=%fused_computation.2 | convolution fusion | flops 75546624 | bytes 4841472 | tf_op jit(solution)/shard_map/dot_general | solution.py:51
  83.7 0.0 reduce-scatter.3.cloned.1.call-update
  83.8 0.0 reduce-scatter.5.cloned.1.call-start
  83.8 0.1 reshape_squeeze.23
  83.9 0.4 fusion.36
  84.3 0.2 fusion.11
  84.5 3.7 %fusion.22 = f32[16,3072]{1,0:T(8,128)} fusion(bf16[768,3072]{1,0:T(8,128)(2,1)} %param.12, bf16[6,2,8,128]{3,2,1,0:T(8,128)(2,1)S(1)} %fusion.11), kind=kOutput, calls=%fused_computation.38 | convolution fusion | flops 75497472 | bytes 4939776 | tf_op jit(solution)/shard_map/dot_general | solution.py:51
  88.3 0.6 fusion.34
  92.5 0.8 dynamic-slice_convert_fusion
  93.4 0.8 fusion.29
  94.2 0.0 reduce-scatter.3.cloned.1.call-done
  94.2 0.8 add_bitcast_fusion
  95.1 3.8 %all_to_all.19 = f32[2,8,1536]{2,1,0:T(8,128)S(1)} all-to-all(f32[2,8,1536]{2,1,0:T(8,128)S(1)} %add_bitcast_fusion), channel_id=1, replica_groups=mesh['groups'=2,'patch'=8,'head'=2] {'head'}, dimensions={0} | all-to-all | bytes 196608 | tf_op jit(solution)/shard_map/all_to_all | solution.py:63
  98.9 5.0 %reduce-scatter.5.cloned.1.call-done = f32[8,3072]{1,0:T(8,128)} async-done(((f32[16,3072]{1,0:T(8,128)}), f32[8,3072]{1,0:T(8,128)}) %reduce-scatter.5.cloned.1.call-update) | async-done | bytes 98320 | tf_op jit(solution)/shard_map/reduce_scatter | solution.py:64
  103.8 1.5 %add_convert_fusion = bf16[8,3072]{1,0:T(8,128)(2,1)} fusion(f32[8,3072]{1,0:T(8,128)S(1)} %bitcast.74, f32[8,3072]{1,0:T(8,128)} %reduce-scatter.5.cloned.1.call-done, f32[3072]{0:T(1024)S(1)} %bitcast.75), kind=kLoop, calls=%fused_computation.29 | loop fusion | flops 73728 | bytes 258048 | tf_op jit(solution)/shard_map/convert_element_type | solution.py:66
  (7 shorter events, 0.0 us)
Async XLA Ops:
  6.5 87.7 %reduce-scatter.3.cloned.1.call-start = ((), (), s32[]{:S(2)}) async-start(), calls=%async_computation.3 | async-start | bytes 147456 | tf_op jit(solution)/shard_map/reduce_scatter | solution.py:54
  80.0 8.3 %copy-start.1 = (s32[2]{0:T(128)S(1)}, s32[2]{0:T(128)}, u32[]{:S(2)}) copy-start(s32[2]{0:T(128)} %param.14) | copy-start | bytes 28
  80.0 14.2 %copy-start = (bf16[16,1536]{1,0:T(8,128)(2,1)S(1)}, bf16[16,1536]{1,0:T(8,128)(2,1)}, u32[]{:S(2)}) copy-start(bf16[16,1536]{1,0:T(8,128)(2,1)} %param.11) | copy-start | bytes 147460
  83.8 20.1 %reduce-scatter.5.cloned.1.call-start = ((), (), s32[]{:S(2)}) async-start(), calls=%async_computation.4 | async-start | bytes 294912 | tf_op jit(solution)/shard_map/reduce_scatter | solution.py:64
Sparse Core Ops, SparseCore 0:
  83.9 8.8 reduce-scatter.2
  95.1 8.7 reduce-scatter.4
where the time goes:
time: 113 us; the launch traced here: 112 us
  blocking collectives  68.1 us (60%)
  between operations  17.8 us (16%)
  matrix products  8.77 us (8%)
  local copies, waits for them, and re-layouts  8.44 us (7%)
  waiting for transfers between devices  5.03 us (4%)
  other arithmetic  4.01 us (4%)
    all_gather x1, blocking collectives, per_device(): first_sets = lax.all_gather(step_pairs[0], 'patch', axis=1, tiled=True)  33 us
    all_gather x1, blocking collectives, per_device(): old_sets = lax.all_gather(stale_pairs, 'patch', axis=1, tiled=True)  31.4 us
    dot_general x2, matrix products, project(): return jnp.dot(attended, out_weight, preferred_element_type=jnp.float32)  7.5 us
    slice x2, local copies, waits for them, and re-layouts, project(): attended = attend(queries[section], pairs[0], pairs[1], usable)  5.91 us
    reduce_scatter x1, waiting for transfers between devices, per_device(): lax.psum_scatter(project(1), 'head', scatter_dimension=0, tiled=True)  4.98 us
    all_to_all x1, blocking collectives, per_device(): lax.all_to_all(state, 'head', split_axis=0, concat_axis=1, tiled=True)  3.79 us
  transfers between devices with their start and end apart: 2, of which 1 were waited for; matrix products, arithmetic and copies ran while one was open for 7% of the time, Pallas kernels for 0%

commit v1 on v0

--- a/solution.py
+++ b/solution.py
@@ -4,6 +4,28 @@
 from jax.sharding import PartitionSpec as P
 
 HDIM = 128
+
+
+def joined_along(blocks, dim):
+    shape = list(blocks.shape[1:])
+    shape[dim] *= blocks.shape[0]
+    return jnp.moveaxis(blocks, 0, dim).reshape(shape)
+
+
+def grow_blocks(x, axis):
+    size = lax.axis_size(axis)
+    blocks = x[None]
+    for level in range(size.bit_length() - 1):
+        bit = 1 << level
+        partner_block = lax.ppermute(blocks, axis, [(i, i ^ bit) for i in range(size)])
+        both = jnp.stack([blocks, partner_block])
+        upper = lax.axis_index(axis) >> level & 1
+        blocks = jnp.where(upper == 0, both, both[::-1]).reshape(-1, *x.shape)
+    return blocks
+
+
+def doubled_up(x, axis, dim):
+    return joined_along(grow_blocks(x, axis), dim)
 
 
 def attend(query_rows, key_rows, value_rows, usable):
@@ -37,7 +59,7 @@
     within = positions % strip_rows
     holder = positions // strip_rows
     usable = (within < lat_rows) | (holder * text_rows + within - lat_rows < text_len[0])
-    old_sets = lax.all_gather(stale_pairs, "patch", axis=1, tiled=True)
+    old_sets = doubled_up(stale_pairs, "patch", 1)
     first_sets = lax.all_gather(step_pairs[0], "patch", axis=1, tiled=True)
     remote_sets = (old_sets, first_sets)
     model_width = out_weight.shape[1]

time: 113 us -> 96.7 us (0.86)
  blocking collectives: 68.1 us -> 35.5 us
  starting transfers between devices: 0.04 us -> 7.31 us
  waiting for transfers between devices: 5.03 us -> 10.3 us
  other arithmetic: 4.01 us -> 6.78 us
    all_gather x1 -> x0, blocking collectives: 31.4 us -> none  [per_device(): old_sets = lax.all_gather(stale_pairs, 'patch', axis=1, tiled=True)]
    ppermute x0 -> x3, starting transfers between devices: none -> 7.26 us  [grow_blocks(): lax.ppermute(blocks, axis, [(i, i ^ bit) for i in range(size)])]
    ppermute x0 -> x3, waiting for transfers between devices: none -> 2.55 us  [grow_blocks(): lax.ppermute(blocks, axis, [(i, i ^ bit) for i in range(size)])]
    another operation x0 -> x4, other arithmetic: none -> 2.19 us  [grow_blocks(): both = jnp.stack([blocks, partner_block])]
    reduce_scatter x1, waiting for transfers between devices: 4.98 us -> 6.42 us  [per_device(): lax.psum_scatter(project(1), 'head', scatter_dimension=0, tiled=True)]
    reduce_scatter x1, waiting for transfers between devices: 0.02 us -> 1.35 us  [per_device(): lax.psum_scatter(project(0).astype(jnp.bfloat16), 'head', scatter_dimensi...]
    all_gather x1, blocking collectives: 33 us -> 31.7 us  [per_device(): first_sets = lax.all_gather(step_pairs[0], 'patch', axis=1, tiled=True)]
  transfers between devices with their start and end apart: 2 -> 5, of which waited for: 1 -> 3; matrix products, arithmetic and copies ran while one was open for 7% -> 10% of each run, Pallas kernels for 0% -> 0%
where the time goes in v1:
time: 96.7 us; the launch traced here: 96 us
  blocking collectives  35.5 us (37%)
  between operations  18.2 us (19%)
  waiting for transfers between devices  10.3 us (11%)
  local copies, waits for them, and re-layouts  9.1 us (9%)
  matrix products  8.76 us (9%)
  starting transfers between devices  7.31 us (8%)
  other arithmetic  6.78 us (7%)
    all_gather x1, blocking collectives, per_device(): first_sets = lax.all_gather(step_pairs[0], 'patch', axis=1, tiled=True)  31.7 us
    dot_general x2, matrix products, project(): return jnp.dot(attended, out_weight, preferred_element_type=jnp.float32)  7.49 us
    ppermute x3, starting transfers between devices, grow_blocks(): lax.ppermute(blocks, axis, [(i, i ^ bit) for i in range(size)])  7.26 us
    reduce_scatter x1, waiting for transfers between devices, per_device(): lax.psum_scatter(project(1), 'head', scatter_dimension=0, tiled=True)  6.42 us
    slice x2, local copies, waits for them, and re-layouts, project(): attended = attend(queries[section], pairs[0], pairs[1], usable)  5.83 us
    all_to_all x1, blocking collectives, per_device(): lax.all_to_all(state, 'head', split_axis=0, concat_axis=1, tiled=True)  3.79 us
    ppermute x3, waiting for transfers between devices, grow_blocks(): lax.ppermute(blocks, axis, [(i, i ^ bit) for i in range(size)])  2.55 us
    another operation x4, other arithmetic, grow_blocks(): both = jnp.stack([blocks, partner_block])  2.19 us
  transfers between devices with their start and end apart: 5, of which 3 were waited for; matrix products, arithmetic and copies ran while one was open for 10% of the time, Pallas kernels for 0%

profile of v1, /device:TPU:0, one launch (start us, length us, event | category | flops | bytes accessed | tf_op | source)
XLA Modules:
  0.0 96.0 jit_solution(15122272511027292682)
XLA Ops:
  6.5 3.0 %collective-permute-start = (bf16[1,2,20,768]{3,1,2,0:T(2,128)(2,1)}, bf16[1,2,20,768]{3,1,2,0:T(2,128)(2,1)S(1)}, u32[]{:S(2)}, u32[]{:S(2)}) collective-permute-start(bf16[1,2,20,768]{3,1,2,0:T(2,128)(2,1)} %bitcast.96), channel_id=1, source_target_pairs={{0,2},{2,0},{4,6},{6,4},{8,10},{10,8},{12,14},{14,12},{1,3},{3,1},... | collective-permute-start | bytes 184328 | tf_op jit(solution)/shard_map/ppermute | solution.py:20
  9.5 1.3 %fusion.36 = (s32[1]{0:T(128)}, s32[1]{0:T(128)}) fusion(s32[2]{0:T(128)} %param.14), kind=kLoop, calls=%fused_computation.66 | loop fusion | bytes 16 | tf_op jit(solution)/shard_map/slice | solution.py:87
  12.8 0.8 dynamic-slice_convert_fusion
  13.6 0.9 slice_bitcast_fusion
  15.1 1.0 %pad_maximum_fusion.2 = bf16[2,1,2,20,768]{4,2,3,1,0:T(2,128)(2,1)S(1)} fusion(bf16[1,1,2,20,768]{4,2,3,1,0:T(2,128)(2,1)S(1)} %bitcast.98, bf16[1,1,2,20,768]{4,2,3,1,0:T(2,128)(2,1)} %bitcast.97), kind=kLoop, calls=%fused_computation.34 | loop fusion | flops 61440 | bytes 245760 | tf_op jit(solution)/shard_map/stack | solution.py:21
  16.3 1.6 %collective-permute-start.1 = (bf16[2,2,20,768]{3,1,2,0:T(2,128)(2,1)S(1)}, bf16[2,2,20,768]{3,1,2,0:T(2,128)(2,1)S(1)}, u32[]{:S(2)}, u32[]{:S(2)}) collective-permute-start(bf16[2,2,20,768]{3,1,2,0:T(2,128)(2,1)S(1)} %get-tuple-element.12), channel_id=1, source_target_pairs={{0,4},{2,6},{4,0},{6,2},{8,12},{10,14},{12,8},{14,10},{1,5},{3,7},... | collective-permute-start | bytes 368648 | tf_op jit(solution)/shard_map/ppermute | solution.py:20
  17.9 0.8 fusion.35
  18.7 2.5 %collective-permute-done.1 = bf16[2,2,20,768]{3,1,2,0:T(2,128)(2,1)S(1)} collective-permute-done((bf16[2,2,20,768]{3,1,2,0:T(2,128)(2,1)S(1)}, bf16[2,2,20,768]{3,1,2,0:T(2,128)(2,1)S(1)}, u32[]{:S(2)}, u32[]{:S(2)}) %collective-permute-start.1) | collective-permute-done | bytes 122912 | tf_op jit(solution)/shard_map/ppermute | solution.py:20
  21.8 2.7 %collective-permute-start.2 = (bf16[4,2,20,768]{3,1,2,0:T(2,128)(2,1)S(1)}, bf16[4,2,20,768]{3,1,2,0:T(2,128)(2,1)S(1)}, u32[]{:S(2)}, u32[]{:S(2)}) collective-permute-start(bf16[4,2,20,768]{3,1,2,0:T(2,128)(2,1)S(1)} %bitcast.91), channel_id=1, source_target_pairs={{0,8},{2,10},{4,12},{6,14},{8,0},{10,2},{12,4},{14,6},{1,9},{3,11}... | collective-permute-start | bytes 737288 | tf_op jit(solution)/shard_map/ppermute | solution.py:20
  26.7 0.8 fusion.31
  27.5 31.7 %all-gather = bf16[1,2,160,768]{3,1,0,2:T(2,128)(2,1)S(1)} all-gather(bf16[1,2,20,768]{3,1,0,2:T(2,128)(2,1)S(1)} %slice_bitcast_fusion), channel_id=2, replica_groups=mesh['groups'=2,'patch'=8,'head'=2] {'patch'}, dimensions={2}, use_global_device_ids=true | all-gather | bytes 552960 | tf_op jit(solution)/shard_map/all_gather | solution.py:63
  59.2 0.7 pad_maximum_fusion
  59.9 0.4 broadcast_select_fusion
  60.3 1.0 %bitcast_dynamic-update-slice_fusion = (bf16[2,160,768]{2,0,1:T(2,128)(2,1)S(1)}, bf16[2,160,768]{2,0,1:T(2,128)(2,1)S(1)}) fusion(bf16[2,160,768]{2,0,1:T(2,128)(2,1)S(1)} %bitcast.89, s32[]{:T(128)S(6)} %select_n.80, bf16[2,2,20,768]{3,1,2,0:T(2,128)(2,1)} %param.10, bf16[2,160,768]{2,0,1:T(2,128)(2,1)S(1)} %bitcast.90), kind=kLoop, calls=%fused_computation.39 | loop fusion | bytes 245764 | tf_op jit(solution)/shard_map/dynamic_update_slice | solution.py:69
  61.3 5.1 %slice_reduce_fusion.1 = (bf16[160,768]{1,0:T(8,128)(2,1)S(1)}, bf16[160,768]{1,0:T(8,128)(2,1)S(1)}, bf16[160,768]{1,0:T(8,128)(2,1)S(1)}, bf16[160,768]{1,0:T(8,128)(2,1)S(1)}) fusion(bf16[2,160,768]{2,0,1:T(2,128)(2,1)S(1)} %get-tuple-element.9, bf16[2,160,768]{2,0,1:T(2,128)(2,1)S(1)} %get-tuple-element.10), kind=kLoop, calls=%fused_computation.19 | loop fusion | bytes 1966080 | tf_op jit(solution)/shard_map/slice | solution.py:72
  66.4 0.4 fusion.37
  67.0 3.7 %convolution_convert_fusion = bf16[16,3072]{1,0:T(8,128)(2,1)} fusion(bf16[768,3072]{1,0:T(8,128)(2,1)} %param.12, bf16[6,2,8,128]{3,2,1,0:T(8,128)(2,1)S(1)} %fusion.10), kind=kOutput, calls=%fused_computation.2 | convolution fusion | flops 75546624 | bytes 4841472 | tf_op jit(solution)/shard_map/dot_general | solution.py:73
  70.8 0.4 fusion.38
  71.4 3.8 %fusion.22 = f32[16,3072]{1,0:T(8,128)} fusion(bf16[768,3072]{1,0:T(8,128)(2,1)} %param.12, bf16[6,2,8,128]{3,2,1,0:T(8,128)(2,1)S(1)} %fusion.11), kind=kOutput, calls=%fused_computation.44 | convolution fusion | flops 75497472 | bytes 4939776 | tf_op jit(solution)/shard_map/dot_general | solution.py:73
  75.2 1.4 %reduce-scatter.3.cloned.1.call-done = bf16[16,1536]{1,0:T(8,128)(2,1)} async-done(((bf16[16,3072]{1,0:T(8,128)(2,1)}), bf16[16,1536]{1,0:T(8,128)(2,1)}) %reduce-scatter.3.cloned.1.call-update) | async-done | bytes 49168 | tf_op jit(solution)/shard_map/reduce_scatter | solution.py:76
  76.6 0.8 add_bitcast_fusion
  77.4 3.8 %all_to_all.19 = f32[2,8,1536]{2,1,0:T(8,128)S(1)} all-to-all(f32[2,8,1536]{2,1,0:T(8,128)S(1)} %add_bitcast_fusion), channel_id=1, replica_groups=mesh['groups'=2,'patch'=8,'head'=2] {'head'}, dimensions={0} | all-to-all | bytes 196608 | tf_op jit(solution)/shard_map/all_to_all | solution.py:85
  81.2 6.4 %reduce-scatter.5.cloned.1.call-done = f32[8,3072]{1,0:T(8,128)} async-done(((f32[16,3072]{1,0:T(8,128)}), f32[8,3072]{1,0:T(8,128)}) %reduce-scatter.5.cloned.1.call-update) | async-done | bytes 98320 | tf_op jit(solution)/shard_map/reduce_scatter | solution.py:86
  87.6 1.5 %add_convert_fusion = bf16[8,3072]{1,0:T(8,128)(2,1)} fusion(f32[8,3072]{1,0:T(8,128)S(1)} %bitcast.93, f32[8,3072]{1,0:T(8,128)} %reduce-scatter.5.cloned.1.call-done, f32[3072]{0:T(1024)S(1)} %bitcast.99), kind=kLoop, calls=%fused_computation.35 | loop fusion | flops 73728 | bytes 258048 | tf_op jit(solution)/shard_map/convert_element_type | solution.py:88
  (16 shorter events, 1.3 us)
Async XLA Ops:
  6.5 70.0 %reduce-scatter.3.cloned.1.call-start = ((), (), s32[]{:S(2)}) async-start(), calls=%async_computation.3 | async-start | bytes 147456 | tf_op jit(solution)/shard_map/reduce_scatter | solution.py:76
  6.5 8.6 %collective-permute-start = (bf16[1,2,20,768]{3,1,2,0:T(2,128)(2,1)}, bf16[1,2,20,768]{3,1,2,0:T(2,128)(2,1)S(1)}, u32[]{:S(2)}, u32[]{:S(2)}) collective-permute-start(bf16[1,2,20,768]{3,1,2,0:T(2,128)(2,1)} %bitcast.96), channel_id=1, source_target_pairs={{0,2},{2,0},{4,6},{6,4},{8,10},{10,8},{12,14},{14,12},{1,3},{3,1},... | collective-permute-start | bytes 184328 | tf_op jit(solution)/shard_map/ppermute | solution.py:20
  16.3 4.9 %collective-permute-start.1 = (bf16[2,2,20,768]{3,1,2,0:T(2,128)(2,1)S(1)}, bf16[2,2,20,768]{3,1,2,0:T(2,128)(2,1)S(1)}, u32[]{:S(2)}, u32[]{:S(2)}) collective-permute-start(bf16[2,2,20,768]{3,1,2,0:T(2,128)(2,1)S(1)} %get-tuple-element.12), channel_id=1, source_target_pairs={{0,4},{2,6},{4,0},{6,2},{8,12},{10,14},{12,8},{14,10},{1,5},{3,7},... | collective-permute-start | bytes 368648 | tf_op jit(solution)/shard_map/ppermute | solution.py:20
  21.8 37.4 %collective-permute-start.2 = (bf16[4,2,20,768]{3,1,2,0:T(2,128)(2,1)S(1)}, bf16[4,2,20,768]{3,1,2,0:T(2,128)(2,1)S(1)}, u32[]{:S(2)}, u32[]{:S(2)}) collective-permute-start(bf16[4,2,20,768]{3,1,2,0:T(2,128)(2,1)S(1)} %bitcast.91), channel_id=1, source_target_pairs={{0,8},{2,10},{4,12},{6,14},{8,0},{10,2},{12,4},{14,6},{1,9},{3,11}... | collective-permute-start | bytes 737288 | tf_op jit(solution)/shard_map/ppermute | solution.py:20
  67.0 9.6 %copy-start = (bf16[16,1536]{1,0:T(8,128)(2,1)S(1)}, bf16[16,1536]{1,0:T(8,128)(2,1)}, u32[]{:S(2)}) copy-start(bf16[16,1536]{1,0:T(8,128)(2,1)} %param.11) | copy-start | bytes 147460
  70.8 16.9 %reduce-scatter.5.cloned.1.call-start = ((), (), s32[]{:S(2)}) async-start(), calls=%async_computation.4 | async-start | bytes 294912 | tf_op jit(solution)/shard_map/reduce_scatter | solution.py:86
Sparse Core Ops, SparseCore 0:
  70.9 5.6 reduce-scatter.2
  78.8 8.7 reduce-scatter.4
